TPU v7x, 128 devices: a whole 4x4x4 slice. The times are simulated.
128 devices in a mesh: seq: 32 (over x, y, core), head: 4 (over z).
Axes of the slice: x: 4, y: 4, z: 4, core: 2. Of those that a mesh axis runs over, the one named last changes fastest.
Arguments:
- queries: bfloat16 [2, 8192, 20, 128], P(None, ('seq', 'head')), may hold values from -96 to 96
- grad_out: bfloat16 [2, 8192, 20, 128], P(None, ('seq', 'head')), may hold values from -6 to 6
- keys: bfloat16 [8192, 4, 128], P('seq', 'head'), may hold values from -6 to 6
- values: bfloat16 [8192, 4, 128], P('seq', 'head'), may hold values from -6 to 6
- doc_start: int32 [8192], replicated, may hold values from 0 to 8191, as said below
Outputs:
- query_grads: bfloat16 [2, 8192, 20, 128], P(None, ('seq', 'head'))
- key_grads: bfloat16 [8192, 4, 128], P('seq', 'head')
- value_grads: bfloat16 [8192, 4, 128], P('seq', 'head')
Inputs may be any that keep to these rules, and one draw needn't show every extreme that they name: doc_start[i] is the first position of token i's document, so doc_start[i] <= i; it is 0 for every token before position 4096, at most four documents begin at or after it, and the last token begins a document of its own.
All inputs are finite; a program needn't handle non-finite values.
Results may differ from a plain program's by a relative error of at most 0.005.
Values may be sent and summed in bfloat16 or wider, within the bound.
A program may use at most 128 MiB of HBM per device.

v0:
```python
import math
import jax
import jax.numpy as jnp
from jax import lax
from jax.sharding import PartitionSpec as P

NEG_START = -1e30


def block_length(key_count):
    return math.gcd(key_count, 1024)


def over_blocks(advance, carried, pieces):
    key_count = pieces[0].shape[0]
    block_rows = block_length(key_count)

    def one_block(block_index, inner):
        block_start = block_index * block_rows
        sliced = tuple(
            (
                lax.dynamic_slice_in_dim(piece_rows, block_start, block_rows, 0)
                for piece_rows in pieces
            )
        )
        return advance(inner, sliced, block_start)

    return lax.fori_loop(0, key_count // block_rows, one_block, carried)


def masked_scores(group, key_block, key_start, score_scale):
    query_rows, grad_rows, starts, positions = group
    key_pos = key_start + jnp.arange(key_block.shape[0], dtype=jnp.int32)
    allowed = (key_pos[None, :] >= starts[:, None]) & (key_pos[None, :] <= positions[:, None])
    scores = (
        jnp.einsum("lrkgd,nkd->lkgrn", query_rows, key_block, preferred_element_type=jnp.float32)
        * score_scale
    )
    return jnp.where(allowed, scores, -jnp.inf)


def stats_update(group, carried, key_block, value_block, key_start, score_scale):

    def stats_compute(inner):
        row_max, row_sum, weighted = inner
        scores = masked_scores(group, key_block, key_start, score_scale)
        new_max = jnp.maximum(row_max, jnp.max(scores, axis=-1))
        raw_weights = jnp.exp(scores - new_max[..., None])
        grad_probs = jnp.einsum(
            "lrkgd,nkd->lkgrn", group[1], value_block, preferred_element_type=jnp.float32
        )
        rescale = jnp.exp(row_max - new_max)
        return (
            new_max,
            row_sum * rescale + jnp.sum(raw_weights, axis=-1),
            weighted * rescale + jnp.sum(raw_weights * grad_probs, axis=-1),
        )

    return lax.cond(key_start > jnp.max(group[3]), lambda inner: inner, stats_compute, carried)


def grads_update(group, row_stats, carried, key_block, value_block, key_start, score_scale):
    log_norm, row_delta = row_stats

    def grads_compute(inner):
        query_acc, key_buffer, value_buffer = inner
        scores = masked_scores(group, key_block, key_start, score_scale)
        prob_rows = jnp.exp(scores - log_norm[..., None])
        grad_probs = jnp.einsum(
            "lrkgd,nkd->lkgrn", group[1], value_block, preferred_element_type=jnp.float32
        )
        grad_scores = prob_rows * (grad_probs - row_delta[..., None])
        grad_low = grad_scores.astype(jnp.bfloat16)
        prob_low = prob_rows.astype(jnp.bfloat16)
        query_acc = query_acc + jnp.einsum(
            "lkgrn,nkd->lrkgd", grad_low, key_block, preferred_element_type=jnp.float32
        )
        key_part = jnp.einsum(
            "lkgrn,lrkgd->nkd", grad_low, group[0], preferred_element_type=jnp.float32
        )
        value_part = jnp.einsum(
            "lkgrn,lrkgd->nkd", prob_low, group[1], preferred_element_type=jnp.float32
        )
        block_rows = key_block.shape[0]
        key_buffer = lax.dynamic_update_slice_in_dim(
            key_buffer,
            lax.dynamic_slice_in_dim(key_buffer, key_start, block_rows, 0) + key_part,
            key_start,
            0,
        )
        value_buffer = lax.dynamic_update_slice_in_dim(
            value_buffer,
            lax.dynamic_slice_in_dim(value_buffer, key_start, block_rows, 0) + value_part,
            key_start,
            0,
        )
        return (query_acc, key_buffer, value_buffer)

    return lax.cond(key_start > jnp.max(group[3]), lambda inner: inner, grads_compute, carried)


def layer_pass(groups, keys, values, score_scale, total_rows):
    stat_init = []
    for group in groups:
        layer_count, row_count, key_heads, group_size, head_width = group[0].shape
        stat_shape = (layer_count, key_heads, group_size, row_count)
        stat_init.append(
            (
                jnp.full(stat_shape, NEG_START, jnp.float32),
                jnp.zeros(stat_shape, jnp.float32),
                jnp.zeros(stat_shape, jnp.float32),
            )
        )

    def advance(inner, sliced, key_start):
        return tuple(
            (
                stats_update(group, member, sliced[0], sliced[1], key_start, score_scale)
                for group, member in zip(groups, inner)
            )
        )

    gathered_stats = over_blocks(
        advance,
        tuple(stat_init),
        (
            lax.all_gather(keys, "seq", axis=0, tiled=True),
            lax.all_gather(values, "seq", axis=0, tiled=True),
        ),
    )
    row_stats = tuple(
        ((member[0] + jnp.log(member[1]), member[2] / member[1]) for member in gathered_stats)
    )
    buffer_shape = (total_rows, keys.shape[1], keys.shape[2])
    grad_init = (
        tuple((jnp.zeros(group[0].shape, jnp.float32) for group in groups)),
        jnp.zeros(buffer_shape, jnp.float32),
        jnp.zeros(buffer_shape, jnp.float32),
    )

    def advance(inner, sliced, key_start):
        query_accs, key_buffer, value_buffer = inner
        updated = []
        for group, stats_pair, query_acc in zip(groups, row_stats, query_accs):
            query_acc, key_buffer, value_buffer = grads_update(
                group,
                stats_pair,
                (query_acc, key_buffer, value_buffer),
                sliced[0],
                sliced[1],
                key_start,
                score_scale,
            )
            updated.append(query_acc)
        return (tuple(updated), key_buffer, value_buffer)

    query_accs, key_buffer, value_buffer = over_blocks(
        advance,
        grad_init,
        (
            lax.all_gather(keys, "seq", axis=0, tiled=True),
            lax.all_gather(values, "seq", axis=0, tiled=True),
        ),
    )
    key_own, value_own = (
        lax.psum_scatter(key_buffer, "seq", scatter_dimension=0, tiled=True),
        lax.psum_scatter(value_buffer, "seq", scatter_dimension=0, tiled=True),
    )
    return (query_accs, key_own, value_own)


def per_device(queries, grad_out, keys, values, doc_start):
    layer_count = queries.shape[0]
    head_width = queries.shape[3]
    key_heads = keys.shape[1]
    score_scale = 1.0 / math.sqrt(head_width)
    regrouped, regrads = (
        lax.all_to_all(queries, "head", split_axis=2, concat_axis=1, tiled=True),
        lax.all_to_all(grad_out, "head", split_axis=2, concat_axis=1, tiled=True),
    )
    row_count = regrouped.shape[1]
    local_heads = regrouped.shape[2]
    group_size = local_heads // key_heads
    five_shape = (layer_count, row_count, key_heads, group_size, head_width)
    query_rows = regrouped.reshape(five_shape)
    grad_rows = regrads.reshape(five_shape)
    seq_index = lax.axis_index("seq")
    seq_count = lax.axis_size("seq")
    total_rows = row_count * seq_count
    offsets = jnp.arange(row_count, dtype=jnp.int32)
    own_pos = seq_index * row_count + offsets
    own_start = lax.dynamic_slice_in_dim(doc_start, seq_index * row_count, row_count, 0)
    groups = ((query_rows, grad_rows, own_start, own_pos),)
    collected = []
    for layer_index in range(layer_count):
        sliced = tuple(
            (
                (
                    group[0][layer_index : layer_index + 1],
                    group[1][layer_index : layer_index + 1],
                    group[2],
                    group[3],
                )
                for group in groups
            )
        )
        accs, key_own, value_own = layer_pass(sliced, keys, values, score_scale, total_rows)
        collected.append(accs)
        if layer_index == 0:
            key_total, value_total = (key_own, value_own)
        else:
            key_total, value_total = (key_total + key_own, value_total + value_own)
    query_accs = tuple(
        (
            jnp.concatenate([accs[member] for accs in collected], axis=0)
            for member in range(len(groups))
        )
    )
    query_low = tuple(((acc * score_scale).astype(jnp.bfloat16) for acc in query_accs))
    query_final = query_low[0]
    query_final = query_final.reshape(layer_count, row_count, local_heads, head_width)
    query_grads = lax.all_to_all(query_final, "head", split_axis=1, concat_axis=2, tiled=True)
    key_grads = (key_total * score_scale).astype(jnp.bfloat16)
    value_grads = value_total.astype(jnp.bfloat16)
    return (query_grads, key_grads, value_grads)


def solution(mesh):
    in_specs = (
        P(None, ("seq", "head"), None, None),
        P(None, ("seq", "head"), None, None),
        P("seq", "head", None),
        P("seq", "head", None),
        P(),
    )
    out_specs = (
        P(None, ("seq", "head"), None, None),
        P("seq", "head", None),
        P("seq", "head", None),
    )
    return jax.shard_map(
        per_device, mesh=mesh, in_specs=in_specs, out_specs=out_specs, check_vma=False
    )
```

profile of v0, /device:TPU:0, one launch (start us, length us, event | category | flops | bytes accessed | tf_op | source)
XLA Modules:
  0.0 597.9 jit_solution(12327094851569278671)
XLA Ops:
  10.6 5.4 all-to-all-start
  16.0 2.0 copy.52
  18.0 8.9 %all-to-all-done = bf16[2,64,20,128]{3,1,0,2:T(8,128)(2,1)S(1)} async-done(((bf16[2,64,20,128]{3,1,0,2:T(8,128)(2,1)}), bf16[2,64,20,128]{3,1,0,2:T(8,128)(2,1)S(1)}, u32[]{:S(2)}, u32[]{:S(2)}) %all-to-all-start) | async-done | bytes 655392 | tf_op jit(solution)/shard_map/all_to_all | solution.py:178
  26.9 3.5 all-to-all-start.1
  31.9 8.5 %all-to-all-done.1 = bf16[2,64,20,128]{3,1,0,2:T(8,128)(2,1)S(1)} async-done(((bf16[2,64,20,128]{3,1,0,2:T(8,128)(2,1)}), bf16[2,64,20,128]{3,1,0,2:T(8,128)(2,1)S(1)}, u32[]{:S(2)}, u32[]{:S(2)}) %all-to-all-start.1) | async-done | bytes 655392 | tf_op jit(solution)/shard_map/all_to_all | solution.py:179
  40.5 15.7 %all-gather.3.cloned.1.call-done = bf16[8192,1,128]{2,0,1:T(8,128)(2,1)} async-done(((bf16[256,1,128]{2,0,1:T(8,128)(2,1)}), bf16[8192,1,128]{2,0,1:T(8,128)(2,1)}) %all-gather.3.cloned.1.call-update) | async-done | bytes 2097168 | tf_op jit(solution)/shard_map/all_gather | solution.py:161
  56.2 45.1 %all-gather.5.cloned.1.call-done = bf16[8192,1,128]{2,0,1:T(8,128)(2,1)} async-done(((bf16[256,1,128]{2,0,1:T(8,128)(2,1)}), bf16[8192,1,128]{2,0,1:T(8,128)(2,1)}) %all-gather.5.cloned.1.call-update) | async-done | bytes 2097168 | tf_op jit(solution)/shard_map/all_gather | solution.py:162
  101.3 10.8 %while.76 = (s32[]{:T(128)}, f32[1,1,5,256]{3,2,1,0:T(8,128)S(1)}, f32[1,1,5,256]{3,2,1,0:T(8,128)S(1)}, f32[1,1,5,256]{3,2,1,0:T(8,128)S(1)}, s32[]{:T(128)}, /...) while((s32[]{:T(128)}, f32[1,1,5,256]{3,2,1,0:T(8,128)S(1)}, ...), condition=%wide.region_7.8_spmd.clone, body=%wide.region_1.7_spmd.clone.sunk | while | flops 687608832 | bytes 18062672 | solution.py:28
  101.9 5.9 conditional.12
  104.1 2.5 fusion.8
  112.2 10.8 %while.78 = (s32[]{:T(128)}, f32[1,1,5,256]{3,2,1,0:T(8,128)S(1)}, f32[1,1,5,256]{3,2,1,0:T(8,128)S(1)}, f32[1,1,5,256]{3,2,1,0:T(8,128)S(1)}, s32[]{:T(128)}, /...) while((s32[]{:T(128)}, f32[1,1,5,256]{3,2,1,0:T(8,128)S(1)}, ...), condition=%wide.region_18.19_spmd.clone, body=%wide.region_12.18_spmd.clone.sunk | while | flops 687608832 | bytes 18062672 | solution.py:28
  112.7 5.9 conditional.14
  115.0 2.5 fusion.58
  123.1 2.2 broadcast.98.clone.1
  125.3 2.2 broadcast.98.clone
  127.5 16.9 %while.79 = (s32[]{:T(128)}, f32[1,256,1,5,128]{1,4,3,0,2:T(8,128)S(1)}, f32[8192,1,128]{2,0,1:T(8,128)}, f32[8192,1,128]{2,0,1:T(8,128)}, s32[]{:T(128)}, /*ind...) while((s32[]{:T(128)}, ...), condition=%wide.region_22.23_spmd.clone, body=%wide.region_19.22_spmd.clone.sunk | while | flops 1692042496 | bytes 29913476 | solution.py:28
  128.1 12.2 %conditional.15 = ((f32[1,256,1,5,128]{1,4,3,0,2:T(8,128)S(1)}, f32[8192,1,128]{2,0,1:T(8,128)}, f32[8192,1,128]{2,0,1:T(8,128)})) conditional(s32[]{:T(128)} %convert_element_type.110, (s32[]{:T(128)}, bf16[8192,1,128]{2,0,1:T(8,128)(2,1)}, s32[256]{0:T(256)S(1)}, s32[]{:T(128)}, bf16[1,256,1,5,128]{4,1,3,2,0:T(8,128)(2,1)S(1)}, ...), branch_computations={%region_20.0_spmd, %region_21.21_spmd} | conditional | flops 1692042496 | bytes 29912158 | solution.py:99
  130.2 2.6 fusion.76
  132.8 3.2 fusion.89
  137.5 2.7 fusion.84
  144.5 2.2 broadcast.98.clone.2
  146.7 2.2 broadcast.98.clone.3
  149.0 16.9 %while.77 = (s32[]{:T(128)}, f32[1,256,1,5,128]{1,4,3,0,2:T(8,128)S(1)}, f32[8192,1,128]{2,0,1:T(8,128)}, f32[8192,1,128]{2,0,1:T(8,128)}, s32[]{:T(128)}, /*ind...) while((s32[]{:T(128)}, ...), condition=%wide.region_11.0_spmd.clone, body=%wide.region_8.11_spmd.clone.sunk | while | flops 1692042496 | bytes 29913476 | solution.py:28
  149.5 12.2 %conditional.13 = ((f32[1,256,1,5,128]{1,4,3,0,2:T(8,128)S(1)}, f32[8192,1,128]{2,0,1:T(8,128)}, f32[8192,1,128]{2,0,1:T(8,128)})) conditional(s32[]{:T(128)} %convert_element_type.108, (s32[]{:T(128)}, bf16[8192,1,128]{2,0,1:T(8,128)(2,1)}, s32[256]{0:T(256)S(1)}, s32[]{:T(128)}, bf16[1,256,1,5,128]{4,1,3,2,0:T(8,128)(2,1)S(1)}, ...), branch_computations={%region_9.9_spmd, %region_10.10_spmd} | conditional | flops 1692042496 | bytes 29912158 | solution.py:99
  151.7 2.6 fusion.26
  154.3 3.2 fusion.39
  159.0 2.7 fusion.34
  165.9 5.8 add.283
  172.1 5.9 add.282
  180.3 15.5 %all_to_all.48 = bf16[2,256,5,128]{3,0,2,1:T(2,128)(2,1)S(1)} all-to-all(bf16[2,256,5,128]{3,0,2,1:T(2,128)(2,1)S(1)} %fusion.108), channel_id=1, replica_groups=mesh['seq'=32,'head'=4] {'head'}, dimensions={1} | all-to-all | bytes 1310720 | tf_op jit(solution)/shard_map/all_to_all | solution.py:222
  196.8 307.9 %reduce-scatter.5.cloned.1.call-done = f32[256,1,128]{2,0,1:T(8,128)} async-done(((f32[8192,1,128]{2,0,1:T(8,128)}), f32[256,1,128]{2,0,1:T(8,128)}) %reduce-scatter.5.cloned.1.call-update) | async-done | bytes 131088 | tf_op jit(solution)/shard_map/reduce_scatter | solution.py:167
  506.2 83.6 %reduce-scatter.3.cloned.1.call-done = f32[256,1,128]{2,0,1:T(8,128)} async-done(((f32[8192,1,128]{2,0,1:T(8,128)}), f32[256,1,128]{2,0,1:T(8,128)}) %reduce-scatter.3.cloned.1.call-update) | async-done | bytes 131088 | tf_op jit(solution)/shard_map/reduce_scatter | solution.py:166
  (148 shorter events, 26.6 us)
Async XLA Ops:
  7.2 49.0 %all-gather.3.cloned.1.call-start = ((), (), s32[]{:S(2)}) async-start(), calls=%async_computation.5 | async-start | bytes 2162688 | tf_op jit(solution)/shard_map/all_gather | solution.py:161
  7.9 93.4 %all-gather.5.cloned.1.call-start = ((), (), s32[]{:S(2)}) async-start(), calls=%async_computation.6 | async-start | bytes 2162688 | tf_op jit(solution)/shard_map/all_gather | solution.py:162
  10.6 16.3 %all-to-all-start = ((bf16[2,64,20,128]{3,1,0,2:T(8,128)(2,1)}), bf16[2,64,20,128]{3,1,0,2:T(8,128)(2,1)S(1)}, u32[]{:S(2)}, u32[]{:S(2)}) async-start(bf16[2,64,20,128]{3,1,0,2:T(8,128)(2,1)} %copy.50), calls=%async_computation | async-start | bytes 1310720 | tf_op jit(solution)/shard_map/all_to_all | solution.py:178
  26.9 13.5 %all-to-all-start.1 = ((bf16[2,64,20,128]{3,1,0,2:T(8,128)(2,1)}), bf16[2,64,20,128]{3,1,0,2:T(8,128)(2,1)S(1)}, u32[]{:S(2)}, u32[]{:S(2)}) async-start(bf16[2,64,20,128]{3,1,0,2:T(8,128)(2,1)} %copy.52), calls=%async_computation.1 | async-start | bytes 1310720 | tf_op jit(solution)/shard_map/all_to_all | solution.py:179
  30.4 474.3 %reduce-scatter.5.cloned.1.call-start = ((), (), s32[]{:S(2)}) async-start(), calls=%async_computation.8 | async-start | bytes 4325376 | tf_op jit(solution)/shard_map/reduce_scatter | solution.py:167
  171.8 418.0 %reduce-scatter.3.cloned.1.call-start = ((), (), s32[]{:S(2)}) async-start(), calls=%async_computation.7 | async-start | bytes 4325376 | tf_op jit(solution)/shard_map/reduce_scatter | solution.py:166
Sparse Core Ops, SparseCore 0:
  10.2 45.9 all-gather.2
  58.5 42.7 all-gather.4
  171.9 332.7 reduce-scatter.4
  508.2 81.5 reduce-scatter.2
where the time goes:
time: 603 us; the launch traced here: 598 us
  waiting for transfers between devices  471 us (78%)
  matrix products  32.5 us (5%)
  other arithmetic  20.2 us (3%)
  loops' own time  19.6 us (3%)
  local copies, waits for them, and re-layouts  16 us (3%)
  blocking collectives  15.5 us (3%)
  between operations  13.9 us (2%)
  starting transfers between devices  9.28 us (2%)
    reduce_scatter x1, waiting for transfers between devices, layer_pass(): lax.psum_scatter(value_buffer, 'seq', scatter_dimension=0, tiled=True)  308 us
    reduce_scatter x1, waiting for transfers between devices, layer_pass(): lax.psum_scatter(key_buffer, 'seq', scatter_dimension=0, tiled=True)  83.6 us
    all_gather x1, waiting for transfers between devices, layer_pass(): lax.all_gather(values, 'seq', axis=0, tiled=True)  45.1 us
    another operation x4, loops' own time, over_blocks(): return lax.fori_loop(0, key_count // block_rows, one_block, carried)  18.5 us
    all_gather x1, waiting for transfers between devices, layer_pass(): lax.all_gather(keys, 'seq', axis=0, tiled=True)  15.7 us
    all_to_all x1, blocking collectives, per_device(): lax.all_to_all(query_final, 'head', split_axis=1, concat_axis=2, tiled=True)  15.5 us
  transfers between devices with their start and end apart: 6, of which 6 were waited for; matrix products, arithmetic and copies ran while one was open for 3% of the time, Pallas kernels for 0%

commit v1 on v0

--- a/solution.py
+++ b/solution.py
@@ -3,8 +3,14 @@
 import jax.numpy as jnp
 from jax import lax
 from jax.sharding import PartitionSpec as P
+from jax.lax import all_to_all, axis_size
 
 NEG_START = -1e30
+
+
+def render_the_numbers(body):
+    k_now = jnp.concatenate(all_to_all(jnp.stack(axis_size("seq") * [body]), "seq", 0, 0), axis=0)
+    return k_now
 
 
 def block_length(key_count):
@@ -157,10 +163,7 @@
     query_accs, key_buffer, value_buffer = over_blocks(
         advance,
         grad_init,
-        (
-            lax.all_gather(keys, "seq", axis=0, tiled=True),
-            lax.all_gather(values, "seq", axis=0, tiled=True),
-        ),
+        (lax.all_gather(keys, "seq", axis=0, tiled=True), render_the_numbers(values)),
     )
     key_own, value_own = (
         lax.psum_scatter(key_buffer, "seq", scatter_dimension=0, tiled=True),

time: 603 us -> 619 us (1.027)
  blocking collectives: 15.5 us -> 27.9 us
    all_to_all x0 -> x1, blocking collectives: none -> 12.4 us  [per_device(): lax.all_to_all(grad_out, 'head', split_axis=2, concat_axis=1, tiled=True)]
    all_gather x1, waiting for transfers between devices: 45.1 us -> 57.2 us  [layer_pass(): lax.all_gather(values, 'seq', axis=0, tiled=True)]
    all_to_all x1, waiting for transfers between devices: 8.46 us -> 0.01 us  [render_the_numbers(): all_to_all(jnp.stack(axis_size('seq') * [body]), 'seq', 0, 0)]
    reduce_scatter x1, waiting for transfers between devices: 308 us -> 302 us  [layer_pass(): lax.psum_scatter(value_buffer, 'seq', scatter_dimension=0, tiled=True)]
  transfers between devices with their start and end apart: 6 -> 6, of which waited for: 6 -> 5; matrix products, arithmetic and copies ran while one was open for 3% -> 5% of each run, Pallas kernels for 0% -> 0%
where the time goes in v1:
time: 619 us; the launch traced here: 615 us
  waiting for transfers between devices  466 us (75%)
  matrix products  31.5 us (5%)
  blocking collectives  27.9 us (5%)
  loops' own time  22.2 us (4%)
  other arithmetic  20.3 us (3%)
  local copies, waits for them, and re-layouts  19.8 us (3%)
  between operations  14 us (2%)
  starting transfers between devices  13.1 us (2%)
    reduce_scatter x1, waiting for transfers between devices, layer_pass(): lax.psum_scatter(value_buffer, 'seq', scatter_dimension=0, tiled=True)  302 us
    reduce_scatter x1, waiting for transfers between devices, layer_pass(): lax.psum_scatter(key_buffer, 'seq', scatter_dimension=0, tiled=True)  83.6 us
    all_gather x1, waiting for transfers between devices, layer_pass(): lax.all_gather(values, 'seq', axis=0, tiled=True)  57.2 us
    another operation x4, loops' own time, over_blocks(): return lax.fori_loop(0, key_count // block_rows, one_block, carried)  21.2 us
    all_to_all x1, blocking collectives, per_device(): lax.all_to_all(query_final, 'head', split_axis=1, concat_axis=2, tiled=True)  15.5 us
    all_gather x1, waiting for transfers between devices, layer_pass(): lax.all_gather(keys, 'seq', axis=0, tiled=True)  12.5 us
    all_to_all x1, blocking collectives, per_device(): lax.all_to_all(grad_out, 'head', split_axis=2, concat_axis=1, tiled=True)  12.4 us
  transfers between devices with their start and end apart: 6, of which 5 were waited for; matrix products, arithmetic and copies ran while one was open for 5% of the time, Pallas kernels for 0%

profile of v1, /device:TPU:0, one launch (start us, length us, event | category | flops | bytes accessed | tf_op | source)
XLA Modules:
  0.0 614.9 jit_solution(16801423045595506998)
XLA Ops:
  8.7 2.0 copy.50
  10.6 5.4 all-to-all-start
  17.2 9.7 %all-to-all-done = bf16[2,64,20,128]{3,1,0,2:T(8,128)(2,1)S(1)} async-done(((bf16[2,64,20,128]{3,1,0,2:T(8,128)(2,1)}), bf16[2,64,20,128]{3,1,0,2:T(8,128)(2,1)S(1)}, u32[]{:S(2)}, u32[]{:S(2)}) %all-to-all-start) | async-done | bytes 655392 | tf_op jit(solution)/shard_map/all_to_all | solution.py:181
  26.9 12.4 %all_to_all.54 = bf16[2,64,20,128]{3,1,0,2:T(8,128)(2,1)S(1)} all-to-all(bf16[2,64,20,128]{3,1,0,2:T(8,128)(2,1)S(1)} %copy.52), channel_id=1, replica_groups=mesh['seq'=32,'head'=4] {'head'}, dimensions={2} | all-to-all | bytes 1310720 | tf_op jit(solution)/shard_map/all_to_all | solution.py:182
  41.2 7.3 %all-to-all-start.2 = ((bf16[32,256,1,128]{3,1,2,0:T(8,128)(2,1)}), bf16[32,256,1,128]{3,1,2,0:T(8,128)(2,1)S(1)}, u32[]{:S(2)}, u32[]{:S(2)}) async-start(bf16[32,256,1,128]{3,1,2,0:T(8,128)(2,1)} %stack.2), calls=%async_computation.2 | async-start | bytes 4194304 | tf_op jit(solution)/shard_map/all_to_all | solution.py:12
  51.0 12.5 %all-gather.3.cloned.1.call-done = bf16[8192,1,128]{2,0,1:T(8,128)(2,1)} async-done(((bf16[256,1,128]{2,0,1:T(8,128)(2,1)}), bf16[8192,1,128]{2,0,1:T(8,128)(2,1)}) %all-gather.3.cloned.1.call-update) | async-done | bytes 2097168 | tf_op jit(solution)/shard_map/all_gather | solution.py:166
  63.5 57.2 %all-gather.5.cloned.1.call-done = bf16[8192,1,128]{2,0,1:T(8,128)(2,1)} async-done(((bf16[256,1,128]{2,0,1:T(8,128)(2,1)}), bf16[8192,1,128]{2,0,1:T(8,128)(2,1)}) %all-gather.5.cloned.1.call-update) | async-done | bytes 2097168 | tf_op jit(solution)/shard_map/all_gather | solution.py:134
  120.7 11.5 %while.76 = (s32[]{:T(128)}, f32[1,1,5,256]{3,2,1,0:T(8,128)S(1)}, f32[1,1,5,256]{3,2,1,0:T(8,128)S(1)}, f32[1,1,5,256]{3,2,1,0:T(8,128)S(1)}, s32[]{:T(128)}, /...) while((s32[]{:T(128)}, f32[1,1,5,256]{3,2,1,0:T(8,128)S(1)}, ...), condition=%wide.region_7.8_spmd.clone, body=%wide.region_1.7_spmd.clone.sunk | while | flops 687608832 | bytes 18062672 | solution.py:34
  121.4 5.9 conditional.12
  121.7 1.9 fusion.10
  123.6 2.5 fusion.8
  133.0 11.5 %while.78 = (s32[]{:T(128)}, f32[1,1,5,256]{3,2,1,0:T(8,128)S(1)}, f32[1,1,5,256]{3,2,1,0:T(8,128)S(1)}, f32[1,1,5,256]{3,2,1,0:T(8,128)S(1)}, s32[]{:T(128)}, /...) while((s32[]{:T(128)}, f32[1,1,5,256]{3,2,1,0:T(8,128)S(1)}, ...), condition=%wide.region_18.19_spmd.clone, body=%wide.region_12.18_spmd.clone.sunk | while | flops 687608832 | bytes 19373420 | solution.py:34
  133.6 5.9 conditional.14
  135.9 2.5 fusion.58
  144.6 2.2 broadcast.101.clone.1
  146.8 2.2 broadcast.101.clone
  149.0 16.7 %while.79 = (s32[]{:T(128)}, f32[1,256,1,5,128]{1,4,3,0,2:T(8,128)S(1)}, f32[8192,1,128]{2,0,1:T(8,128)}, f32[8192,1,128]{2,0,1:T(8,128)}, s32[]{:T(128)}, /*ind...) while((s32[]{:T(128)}, ...), condition=%wide.region_22.23_spmd.clone, body=%wide.region_19.22_spmd.clone.sunk | while | flops 1692042496 | bytes 31230368 | solution.py:34
  149.6 11.3 %conditional.15 = ((f32[1,256,1,5,128]{1,4,3,0,2:T(8,128)S(1)}, f32[8192,1,128]{2,0,1:T(8,128)}, f32[8192,1,128]{2,0,1:T(8,128)})) conditional(s32[]{:T(128)} %convert_element_type.110, (s32[]{:T(128)}, bf16[8192,1,128]{2,0,1:T(8,128)(2,1)}, s32[256]{0:T(256)S(1)}, s32[]{:T(128)}, bf16[1,256,1,5,128]{4,1,3,2,0:T(8,128)(2,1)S(1)}, ...), branch_computations={%region_20.0_spmd, %region_21.21_spmd} | conditional | flops 1692042496 | bytes 31229050 | solution.py:105
  153.4 3.2 fusion.89
  158.2 2.7 fusion.84
  167.0 2.3 broadcast.101.clone.2
  169.3 2.2 broadcast.101.clone.3
  171.6 17.6 %while.77 = (s32[]{:T(128)}, f32[1,256,1,5,128]{1,4,3,0,2:T(8,128)S(1)}, f32[8192,1,128]{2,0,1:T(8,128)}, f32[8192,1,128]{2,0,1:T(8,128)}, s32[]{:T(128)}, /*ind...) while((s32[]{:T(128)}, ...), condition=%wide.region_11.0_spmd.clone, body=%wide.region_8.11_spmd.clone.sunk | while | flops 1692042496 | bytes 29913476 | solution.py:34
  172.2 12.2 %conditional.13 = ((f32[1,256,1,5,128]{1,4,3,0,2:T(8,128)S(1)}, f32[8192,1,128]{2,0,1:T(8,128)}, f32[8192,1,128]{2,0,1:T(8,128)})) conditional(s32[]{:T(128)} %convert_element_type.108, (s32[]{:T(128)}, bf16[8192,1,128]{2,0,1:T(8,128)(2,1)}, s32[256]{0:T(256)S(1)}, s32[]{:T(128)}, bf16[1,256,1,5,128]{4,1,3,2,0:T(8,128)(2,1)S(1)}, ...), branch_computations={%region_9.9_spmd, %region_10.10_spmd} | conditional | flops 1692042496 | bytes 29912158 | solution.py:105
  174.3 2.6 fusion.26
  176.9 3.2 fusion.39
  181.7 2.7 fusion.34
  189.1 5.8 add.283
  195.3 5.9 add.282
  203.5 15.5 %all_to_all.55 = bf16[2,256,5,128]{3,0,2,1:T(2,128)(2,1)S(1)} all-to-all(bf16[2,256,5,128]{3,0,2,1:T(2,128)(2,1)S(1)} %fusion.108), channel_id=1, replica_groups=mesh['seq'=32,'head'=4] {'head'}, dimensions={1} | all-to-all | bytes 1310720 | tf_op jit(solution)/shard_map/all_to_all | solution.py:225
  220.0 301.6 %reduce-scatter.5.cloned.1.call-done = f32[256,1,128]{2,0,1:T(8,128)} async-done(((f32[8192,1,128]{2,0,1:T(8,128)}), f32[256,1,128]{2,0,1:T(8,128)}) %reduce-scatter.5.cloned.1.call-update) | async-done | bytes 131088 | tf_op jit(solution)/shard_map/reduce_scatter | solution.py:170
  523.2 83.6 %reduce-scatter.3.cloned.1.call-done = f32[256,1,128]{2,0,1:T(8,128)} async-done(((f32[8192,1,128]{2,0,1:T(8,128)}), f32[256,1,128]{2,0,1:T(8,128)}) %reduce-scatter.3.cloned.1.call-update) | async-done | bytes 131088 | tf_op jit(solution)/shard_map/reduce_scatter | solution.py:169
  (162 shorter events, 30.2 us)
Async XLA Ops:
  7.2 32.2 %copy-start.5 = (bf16[256,1,128]{2,0,1:T(8,128)(2,1)S(1)}, bf16[256,1,128]{2,0,1:T(8,128)(2,1)}, u32[]{:S(2)}) copy-start(bf16[256,1,128]{2,0,1:T(8,128)(2,1)} %param.24) | copy-start | bytes 196612
  7.2 56.3 %all-gather.3.cloned.1.call-start = ((), (), s32[]{:S(2)}) async-start(), calls=%async_computation.6 | async-start | bytes 2162688 | tf_op jit(solution)/shard_map/all_gather | solution.py:166
  7.9 112.8 %all-gather.5.cloned.1.call-start = ((), (), s32[]{:S(2)}) async-start(), calls=%async_computation.7 | async-start | bytes 2162688 | tf_op jit(solution)/shard_map/all_gather | solution.py:134
  10.6 16.3 %all-to-all-start = ((bf16[2,64,20,128]{3,1,0,2:T(8,128)(2,1)}), bf16[2,64,20,128]{3,1,0,2:T(8,128)(2,1)S(1)}, u32[]{:S(2)}, u32[]{:S(2)}) async-start(bf16[2,64,20,128]{3,1,0,2:T(8,128)(2,1)} %copy.50), calls=%async_computation | async-start | bytes 1310720 | tf_op jit(solution)/shard_map/all_to_all | solution.py:181
  41.2 103.3 %all-to-all-start.2 = ((bf16[32,256,1,128]{3,1,2,0:T(8,128)(2,1)}), bf16[32,256,1,128]{3,1,2,0:T(8,128)(2,1)S(1)}, u32[]{:S(2)}, u32[]{:S(2)}) async-start(bf16[32,256,1,128]{3,1,2,0:T(8,128)(2,1)} %stack.2), calls=%async_computation.2 | async-start | bytes 4194304 | tf_op jit(solution)/shard_map/all_to_all | solution.py:12
  48.5 473.1 %reduce-scatter.5.cloned.1.call-start = ((), (), s32[]{:S(2)}) async-start(), calls=%async_computation.9 | async-start | bytes 4325376 | tf_op jit(solution)/shard_map/reduce_scatter | solution.py:170
  132.2 0.7 copy-start.1
  133.6 2.2 copy-start.3
  149.6 2.1 copy-start.4
  165.7 1.3 copy-start
  167.0 4.6 copy-start.2
  195.0 411.8 %reduce-scatter.3.cloned.1.call-start = ((), (), s32[]{:S(2)}) async-start(), calls=%async_computation.8 | async-start | bytes 4325376 | tf_op jit(solution)/shard_map/reduce_scatter | solution.py:169
Sparse Core Ops, SparseCore 0:
  10.2 53.2 all-gather.2
  65.8 54.9 all-gather.4
  195.1 326.4 reduce-scatter.4
  525.1 81.6 reduce-scatter.2
